TPU v7x, 256 devices: a whole 4x4x8 slice. The times are simulated.
256 devices in a mesh: row: 8 (over x_hi, y), col: 32 (over z, x_lo, core).
Axes of the slice: x: 4 (x_hi: 2, x_lo: 2; x = x_hi * 2 + x_lo), y: 4, z: 8, core: 2. Of those that a mesh axis runs over, the one named last changes fastest.
Arguments:
- samples: float32 [1024, 64, 128], P(('row', 'col')), may hold values from -6 to 6
- omega: float32 [8, 32, 100, 128, 128], P('row', 'col'), may hold values from -0.12 to 2.12
- block_rows: int32 [8, 32, 100], P('row', 'col'), may hold values from -1 to 1023, as said below
- block_cols: int32 [8, 32, 100], P('row', 'col'), may hold values from -1 to 1023, as said below
Outputs:
- omega_next: float32 [8, 32, 100, 128, 128], P('row', 'col')
Inputs may be any that keep to these rules, and one draw needn't show every extreme that they name: `block_rows`: slots 0 to 3 of the device at (a, b) hold the diagonal blocks I = J = (a * 32 + b) * 4 + k in order of k; the other slots hold distinct off-diagonal blocks whose block row lies in a * 1024 / 8 up to (a + 1) * 1024 / 8 - 1 and whose block column J has (J // 4) % 32 = b; live slots come first and -1 fills the rest; some device has all 100 slots live. `block_cols`: -1 exactly where block_rows is -1.
All inputs are finite; a program needn't handle non-finite values.
Results may differ from a plain program's by a relative error of at most 0.0003.
Values sent between devices are 32-bit elements; how exact they have to be, the bound alone decides.
A program may use at most 128 MiB of HBM per device.

v0:
```python
import jax
import jax.numpy as jnp
from jax import lax
from jax.sharding import PartitionSpec as P

ITERS = 2
STEP = 0.5
PENALTY = 0.1


def gradient_blocks(left_totals, right_samples, left_samples, right_totals, sample_count):
    forward = jnp.einsum(
        "snb,snk->sbk", left_totals, right_samples, precision=lax.Precision.HIGHEST
    )
    mirrored = jnp.einsum(
        "snb,snk->sbk", left_samples, right_totals, precision=lax.Precision.HIGHEST
    )
    return (forward + mirrored) * (0.5 / sample_count)


def proximal(current, grad, active, on_diagonal):
    stepped = current - STEP * grad
    eye_mask = jnp.eye(current.shape[-1], dtype=bool)[None] & on_diagonal[:, None, None]
    shrunk = jnp.sign(stepped) * jnp.maximum(jnp.abs(stepped) - STEP * PENALTY, 0.0)
    lifted = 0.5 * (stepped + jnp.sqrt(stepped * stepped + 4.0 * STEP))
    updated = jnp.where(eye_mask, lifted, shrunk)
    return jnp.where(active[:, None, None], updated, 0.0)


def shards(samples, omega, block_rows, block_cols):
    col_count = lax.axis_size("col")
    row_index = lax.axis_index("row")
    slab_blocks = samples.shape[0]
    sample_count = samples.shape[1]
    width = samples.shape[2]
    group_rows = slab_blocks * col_count
    current = omega[0, 0]
    row_ids = block_rows[0, 0]
    col_ids = block_cols[0, 0]
    active = row_ids >= 0
    local_rows = jnp.where(active, row_ids - row_index * group_rows, -1)
    safe_rows = jnp.maximum(local_rows, 0)
    slab_ids = col_ids // slab_blocks
    local_cols = jnp.where(active, slab_ids // col_count * slab_blocks + col_ids % slab_blocks, 0)
    on_diagonal = active & (row_ids == col_ids)
    row_samples = lax.all_gather(samples, "col", axis=0, tiled=True)
    col_samples = lax.all_gather(samples, "row", axis=0, tiled=True)
    picked_cols = col_samples[local_cols]
    picked_rows = row_samples[safe_rows]
    for iteration in range(ITERS):
        products = jnp.einsum("snk,sbk->snb", picked_cols, current, precision=lax.Precision.HIGHEST)
        flattened = products.reshape(products.shape[0], -1)

        def rows_term(offset, length, flattened=flattened):
            selector = (local_rows[None, :] == jnp.arange(length)[:, None]).astype(jnp.float32)
            summed_part = jnp.dot(selector, flattened, precision=lax.Precision.HIGHEST)
            return summed_part.reshape(length, sample_count, width)

        own_totals = lax.psum_scatter(
            rows_term(jnp.int32(0), slab_blocks * lax.axis_size("col")),
            "col",
            scatter_dimension=0,
            tiled=True,
        )
        row_totals = lax.all_gather(own_totals, "col", axis=0, tiled=True)
        col_totals = lax.all_gather(own_totals, "row", axis=0, tiled=True)
        grad = gradient_blocks(
            row_totals[safe_rows], picked_cols, picked_rows, col_totals[local_cols], sample_count
        )
        current = proximal(current, grad, active, on_diagonal)
    return current[None, None]


def solution(mesh):
    return jax.shard_map(
        shards,
        mesh=mesh,
        in_specs=(
            P(("row", "col"), None, None),
            P("row", "col", None, None, None),
            P("row", "col", None),
            P("row", "col", None),
        ),
        out_specs=P("row", "col", None, None, None),
        check_vma=False,
    )
```

profile of v0, /device:TPU:1, one launch (start us, length us, event | category | flops | bytes accessed | tf_op | source)
XLA Modules:
  0.0 751.3 jit_solution(15371741248821138310)
XLA Ops:
  6.5 0.0 all-gather.7.cloned.1.call-start
  6.5 0.7 all-gather.7.cloned.1.call-update
  7.3 0.0 reduce-scatter.3.cloned.1.call-start
  7.3 0.7 fusion.16
  8.0 0.7 bitcast_select_fusion.2
  8.7 54.9 %all-gather.7.cloned.1.call-done = f32[32,64,128]{2,1,0:T(8,128)} async-done(((f32[4,64,128]{2,1,0:T(8,128)}), f32[32,64,128]{2,1,0:T(8,128)}) %all-gather.7.cloned.1.call-update) | async-done | bytes 1048592 | tf_op jit(solution)/shard_map/all_gather | solution.py:47
  63.6 2.0 gather_fusion
  65.6 14.8 %fusion.3 = f32[100,64,128]{2,1,0:T(8,128)S(1)} fusion(f32[100,64,128]{2,1,0:T(8,128)S(1)} %gather_fusion, f32[1,1,100,128,128]{4,3,2,1,0:T(8,128)} %param.5), kind=kOutput, calls=%fused_computation.12 | convolution fusion | flops 1258291200 | bytes 13107200 | tf_op jit(solution)/shard_map/snk,sbk->snb/dot_general | solution.py:51
  80.4 0.4 slice_bitcast_fusion.1
  80.8 4.1 fusion.7
  84.9 4.4 copy.16
  89.4 0.0 copy-start.5
  89.4 0.0 copy-start.6
  89.4 0.0 reduce-scatter.3.cloned.1.call-update
  89.4 0.0 all-gather.11.cloned.1.call-start
  89.5 0.7 all-gather.11.cloned.1.call-update
  90.1 0.0 all-gather.13.cloned.1.call-start
  90.2 121.1 %reduce-scatter.3.cloned.1.call-done = f32[4,64,128]{2,1,0:T(8,128)} async-done(((f32[128,64,128]{2,1,0:T(8,128)}), f32[4,64,128]{2,1,0:T(8,128)}) %reduce-scatter.3.cloned.1.call-update) | async-done | bytes 131088 | tf_op jit(solution)/shard_map/reduce_scatter | solution.py:59
  211.3 0.0 all-gather.13.cloned.1.call-update
  211.3 0.0 all-gather.9.cloned.1.call-start
  211.4 0.5 all-gather.9.cloned.1.call-update
  211.9 0.3 reduce-scatter.5.cloned.1.call-start
  212.2 0.0 copy-done.5
  212.3 0.0 copy-done.6
  212.3 69.6 %all-gather.11.cloned.1.call-done = f32[128,64,128]{2,1,0:T(8,128)} async-done(((f32[4,64,128]{2,1,0:T(8,128)}), f32[128,64,128]{2,1,0:T(8,128)}) %all-gather.11.cloned.1.call-update) | async-done | bytes 4194320 | tf_op jit(solution)/shard_map/all_gather | solution.py:46
  281.8 4.6 gather_fusion.2
  286.4 47.3 %all-gather.13.cloned.1.call-done = f32[32,64,128]{2,1,0:T(8,128)} async-done(((f32[4,64,128]{2,1,0:T(8,128)}), f32[32,64,128]{2,1,0:T(8,128)}) %all-gather.13.cloned.1.call-update) | async-done | bytes 1048592 | tf_op jit(solution)/shard_map/all_gather | solution.py:66
  333.7 3.6 gather_fusion.3
  337.3 65.5 %all-gather.9.cloned.1.call-done = f32[128,64,128]{2,1,0:T(8,128)} async-done(((f32[4,64,128]{2,1,0:T(8,128)}), f32[128,64,128]{2,1,0:T(8,128)}) %all-gather.9.cloned.1.call-update) | async-done | bytes 4194320 | tf_op jit(solution)/shard_map/all_gather | solution.py:65
  402.8 4.7 gather_fusion.1
  407.5 0.0 copy-start.1
  407.5 0.0 copy-start.4
  407.5 12.5 %fusion.19 = f32[100,128,128]{2,1,0:T(8,128)S(1)} fusion(f32[100,64,128]{2,1,0:T(8,128)} %gather_fusion.1, f32[100,64,128]{2,1,0:T(8,128)S(1)} %gather_fusion), kind=kOutput, calls=%fused_computation.48 | convolution fusion | flops 1258291200 | bytes 13107200 | tf_op jit(solution)/shard_map/snb,snk->sbk/dot_general | solution.py:12
  420.0 0.0 copy-done.1
  420.0 0.0 copy-done.4
  420.0 19.4 %fusion = f32[100,128,128]{2,1,0:T(8,128)S(1)} fusion(f32[1,1,100,128,128]{4,3,2,1,0:T(8,128)} %param.5, f32[100,128,128]{2,1,0:T(8,128)S(1)} %fusion.19, pred[100]{0:T(512)(128)(4,1)S(1)} %fusion.18, pred[128,128]{1,0:T(8,128)(4,1)S(1)} %iota_compare_fusion, pred[100]{0:T(512)(128)(4,1)S(1)} %bitcast_and_fusion, f32[100,64,128]{2,1,0:T(8,128)S(1)} %copy-done.1, ...), kind=kOutput, calls=%fused_computation.8 | convolution fusion | flops 1282867200 | bytes 26230984 | tf_op jit(solution)/shard_map/snb,snk->sbk/dot_general | solution.py:15
  439.4 0.0 copy-start
  439.4 13.0 %fusion.20 = f32[100,64,128]{2,1,0:T(8,128)S(1)} fusion(f32[100,64,128]{2,1,0:T(8,128)S(1)} %gather_fusion, f32[100,128,128]{2,1,0:T(8,128)S(1)} %fusion), kind=kOutput, calls=%fused_computation.49 | convolution fusion | flops 1258291200 | bytes 13107200 | tf_op jit(solution)/shard_map/snk,sbk->snb/dot_general | solution.py:51
  452.3 0.0 copy-done
  452.3 0.4 slice_bitcast_fusion
  452.8 4.1 fusion.5
  456.9 4.7 copy.18
  461.6 0.0 reduce-scatter.5.cloned.1.call-update
  461.6 0.0 all-gather.17.cloned.1.call-start
  461.7 121.0 %reduce-scatter.5.cloned.1.call-done = f32[4,64,128]{2,1,0:T(8,128)} async-done(((f32[128,64,128]{2,1,0:T(8,128)}), f32[4,64,128]{2,1,0:T(8,128)}) %reduce-scatter.5.cloned.1.call-update) | async-done | bytes 131088 | tf_op jit(solution)/shard_map/reduce_scatter | solution.py:59
  582.7 0.0 all-gather.17.cloned.1.call-update
  582.7 0.0 all-gather.15.cloned.1.call-start
  582.7 0.7 all-gather.15.cloned.1.call-update
  583.4 53.3 %all-gather.17.cloned.1.call-done = f32[32,64,128]{2,1,0:T(8,128)} async-done(((f32[4,64,128]{2,1,0:T(8,128)}), f32[32,64,128]{2,1,0:T(8,128)}) %all-gather.17.cloned.1.call-update) | async-done | bytes 1048592 | tf_op jit(solution)/shard_map/all_gather | solution.py:66
  636.8 3.7 gather_fusion.5
  640.5 65.5 %all-gather.15.cloned.1.call-done = f32[128,64,128]{2,1,0:T(8,128)} async-done(((f32[4,64,128]{2,1,0:T(8,128)}), f32[128,64,128]{2,1,0:T(8,128)}) %all-gather.15.cloned.1.call-update) | async-done | bytes 4194320 | tf_op jit(solution)/shard_map/all_gather | solution.py:65
  706.0 4.7 gather_fusion.4
  710.7 0.0 copy-start.2
  710.7 0.0 copy-start.3
  710.7 12.5 %fusion.21 = f32[100,128,128]{2,1,0:T(8,128)S(1)} fusion(f32[100,64,128]{2,1,0:T(8,128)} %gather_fusion.4, f32[100,64,128]{2,1,0:T(8,128)S(1)} %gather_fusion), kind=kOutput, calls=%fused_computation.50 | convolution fusion | flops 1258291200 | bytes 13107200 | tf_op jit(solution)/shard_map/snb,snk->sbk/dot_general | solution.py:12
  723.2 0.0 copy-done.2
  723.2 0.0 copy-done.3
  723.2 20.7 %fusion.2 = f32[1,1,100,128,128]{4,3,2,1,0:T(8,128)} fusion(f32[100,128,128]{2,1,0:T(8,128)} %copy-done, f32[100,128,128]{2,1,0:T(8,128)S(1)} %fusion.21, pred[100]{0:T(512)(128)(4,1)S(1)} %fusion.18, pred[128,128]{1,0:T(8,128)(4,1)S(1)} %iota_compare_fusion, pred[100]{0:T(512)(128)(4,1)S(1)} %bitcast_and_fusion, f32[100,64,128]{2,1,0:T(8,128)S(1)} %copy-done.2, ...), kind=kOutput, calls=%fused_computation.10 | convolution fusion | flops 1282867200 | bytes 26230984 | tf_op jit(solution)/shard_map/snb,snk->sbk/dot_general | solution.py:15
  (5 shorter events, 0.0 us)
Async XLA Ops:
  6.5 57.0 %all-gather.7.cloned.1.call-start = ((), (), s32[]{:S(2)}) async-start(), calls=%async_computation.2 | async-start | bytes 1179648 | tf_op jit(solution)/shard_map/all_gather | solution.py:47
  7.3 204.1 %reduce-scatter.3.cloned.1.call-start = ((), (), s32[]{:S(2)}) async-start(), calls=%async_computation.3 | async-start | bytes 4325376 | tf_op jit(solution)/shard_map/reduce_scatter | solution.py:59
  89.4 122.9 %copy-start.5 = (s32[1,1,100]{2,1,0:T(1,128)S(1)}, s32[1,1,100]{2,1,0:T(1,128)}, u32[]{:S(2)}) copy-start(s32[1,1,100]{2,1,0:T(1,128)} %param.6) | copy-start | bytes 1204
  89.4 122.9 %copy-start.6 = (s32[1,1,100]{2,1,0:T(1,128)S(1)}, s32[1,1,100]{2,1,0:T(1,128)}, u32[]{:S(2)}) copy-start(s32[1,1,100]{2,1,0:T(1,128)} %param.7) | copy-start | bytes 1204
  89.4 192.4 %all-gather.11.cloned.1.call-start = ((), (), s32[]{:S(2)}) async-start(), calls=%async_computation.5 | async-start | bytes 4325376 | tf_op jit(solution)/shard_map/all_gather | solution.py:46
  90.1 243.6 %all-gather.13.cloned.1.call-start = ((), (), s32[]{:S(2)}) async-start(), calls=%async_computation.6 | async-start | bytes 1179648 | tf_op jit(solution)/shard_map/all_gather | solution.py:66
  211.3 191.4 %all-gather.9.cloned.1.call-start = ((), (), s32[]{:S(2)}) async-start(), calls=%async_computation.4 | async-start | bytes 4325376 | tf_op jit(solution)/shard_map/all_gather | solution.py:65
  211.9 370.7 %reduce-scatter.5.cloned.1.call-start = ((), (), s32[]{:S(2)}) async-start(), calls=%async_computation.7 | async-start | bytes 4325376 | tf_op jit(solution)/shard_map/reduce_scatter | solution.py:59
  407.5 12.5 %copy-start.1 = (f32[100,64,128]{2,1,0:T(8,128)S(1)}, f32[100,64,128]{2,1,0:T(8,128)}, u32[]{:S(2)}) copy-start(f32[100,64,128]{2,1,0:T(8,128)} %gather_fusion.2) | copy-start | bytes 9830404
  407.5 12.5 %copy-start.4 = (f32[100,64,128]{2,1,0:T(8,128)S(1)}, f32[100,64,128]{2,1,0:T(8,128)}, u32[]{:S(2)}) copy-start(f32[100,64,128]{2,1,0:T(8,128)} %gather_fusion.3) | copy-start | bytes 9830404
  439.4 13.0 %copy-start = (f32[100,128,128]{2,1,0:T(8,128)}, f32[100,128,128]{2,1,0:T(8,128)S(1)}, u32[]{:S(2)}) copy-start(f32[100,128,128]{2,1,0:T(8,128)S(1)} %fusion) | copy-start | bytes 19660804
  461.6 175.1 %all-gather.17.cloned.1.call-start = ((), (), s32[]{:S(2)}) async-start(), calls=%async_computation.9 | async-start | bytes 1179648 | tf_op jit(solution)/shard_map/all_gather | solution.py:66
  582.7 123.3 %all-gather.15.cloned.1.call-start = ((), (), s32[]{:S(2)}) async-start(), calls=%async_computation.8 | async-start | bytes 4325376 | tf_op jit(solution)/shard_map/all_gather | solution.py:65
  710.7 12.5 %copy-start.2 = (f32[100,64,128]{2,1,0:T(8,128)S(1)}, f32[100,64,128]{2,1,0:T(8,128)}, u32[]{:S(2)}) copy-start(f32[100,64,128]{2,1,0:T(8,128)} %gather_fusion.2) | copy-start | bytes 9830404
  710.7 12.5 %copy-start.3 = (f32[100,64,128]{2,1,0:T(8,128)S(1)}, f32[100,64,128]{2,1,0:T(8,128)}, u32[]{:S(2)}) copy-start(f32[100,64,128]{2,1,0:T(8,128)} %gather_fusion.5) | copy-start | bytes 9830404
Sparse Core Ops, SparseCore 0:
  10.0 53.5 all-gather.6
  89.5 121.7 reduce-scatter.2
  213.2 68.5 all-gather.10
  284.3 49.3 all-gather.12
  335.4 67.3 all-gather.8
  461.7 120.8 reduce-scatter.4
  585.3 51.3 all-gather.16
  638.6 67.3 all-gather.14
where the time goes:
time: 760 us; the launch traced here: 751 us
  waiting for transfers between devices  601 us (79%)
  matrix products  101 us (13%)
  local copies, waits for them, and re-layouts  33.3 us (4%)
  between operations  14.1 us (2%)
    reduce_scatter x2, waiting for transfers between devices, shards(): lax.psum_scatter(rows_term(jnp.int32(0), slab_blocks * lax.axis_size('col...  242 us
    all_gather x2, waiting for transfers between devices, shards(): row_totals = lax.all_gather(own_totals, 'col', axis=0, tiled=True)  131 us
    all_gather x2, waiting for transfers between devices, shards(): col_totals = lax.all_gather(own_totals, 'row', axis=0, tiled=True)  101 us
    all_gather x1, waiting for transfers between devices, shards(): row_samples = lax.all_gather(samples, 'col', axis=0, tiled=True)  69.6 us
    all_gather x1, waiting for transfers between devices, shards(): col_samples = lax.all_gather(samples, 'row', axis=0, tiled=True)  54.9 us
    dot_general x2, matrix products, gradient_blocks(): jnp.einsum('snb,snk->sbk', left_samples, right_totals, precision=lax.Prec...  40.1 us
    dot_general x2, matrix products, shards(): jnp.einsum('snk,sbk->snb', picked_cols, current, precision=lax.Precision....  27.8 us
    dot_general x2, matrix products, gradient_blocks(): jnp.einsum('snb,snk->sbk', left_totals, right_samples, precision=lax.Prec...  25 us
  transfers between devices with their start and end apart: 8, of which 8 were waited for; matrix products, arithmetic and copies ran while one was open for 2% of the time, Pallas kernels for 0%

commit v1 on v0

--- a/solution.py
+++ b/solution.py
@@ -43,7 +43,10 @@
     slab_ids = col_ids // slab_blocks
     local_cols = jnp.where(active, slab_ids // col_count * slab_blocks + col_ids % slab_blocks, 0)
     on_diagonal = active & (row_ids == col_ids)
-    row_samples = lax.all_gather(samples, "col", axis=0, tiled=True)
+    size = lax.axis_size("col")
+    blocks = jnp.stack([samples for _ in range(size)])
+    blocks = lax.all_to_all(blocks, "col", split_axis=0, concat_axis=0)
+    row_samples = jnp.concatenate(blocks, axis=0)
     col_samples = lax.all_gather(samples, "row", axis=0, tiled=True)
     picked_cols = col_samples[local_cols]
     picked_rows = row_samples[safe_rows]

time: 760 us -> 715 us (0.941)
  waiting for transfers between devices: 601 us -> 544 us
  starting transfers between devices: 0.49 us -> 9.29 us
    all_to_all x0 -> x1, waiting for transfers between devices: none -> 101 us  [shards(): blocks = lax.all_to_all(blocks, 'col', split_axis=0, concat_axis=0)]
    all_gather x1 -> x0, waiting for transfers between devices: 69.6 us -> none  [shards(): row_samples = lax.all_gather(samples, 'col', axis=0, tiled=True)]
    all_gather x2, waiting for transfers between devices: 101 us -> 52.9 us  [shards(): col_totals = lax.all_gather(own_totals, 'row', axis=0, tiled=True)]
    all_gather x2, waiting for transfers between devices: 131 us -> 90.5 us  [shards(): row_totals = lax.all_gather(own_totals, 'col', axis=0, tiled=True)]
    all_to_all x0 -> x1, starting transfers between devices: none -> 9.05 us  [shards(): blocks = lax.all_to_all(blocks, 'col', split_axis=0, concat_axis=0)]
  transfers between devices with their start and end apart: 8 -> 8, of which waited for: 8 -> 7; matrix products, arithmetic and copies ran while one was open for 2% -> 2% of each run, Pallas kernels for 0% -> 0%
where the time goes in v1:
time: 715 us; the launch traced here: 706 us
  waiting for transfers between devices  544 us (76%)
  matrix products  101 us (14%)
  local copies, waits for them, and re-layouts  35.9 us (5%)
  between operations  14.1 us (2%)
  starting transfers between devices  9.29 us (1%)
    reduce_scatter x2, waiting for transfers between devices, shards(): lax.psum_scatter(rows_term(jnp.int32(0), slab_blocks * lax.axis_size('col...  243 us
    all_to_all x1, waiting for transfers between devices, shards(): blocks = lax.all_to_all(blocks, 'col', split_axis=0, concat_axis=0)  101 us
    all_gather x2, waiting for transfers between devices, shards(): row_totals = lax.all_gather(own_totals, 'col', axis=0, tiled=True)  90.5 us
    all_gather x1, waiting for transfers between devices, shards(): col_samples = lax.all_gather(samples, 'row', axis=0, tiled=True)  54.9 us
    all_gather x2, waiting for transfers between devices, shards(): col_totals = lax.all_gather(own_totals, 'row', axis=0, tiled=True)  52.9 us
    dot_general x2, matrix products, gradient_blocks(): jnp.einsum('snb,snk->sbk', left_samples, right_totals, precision=lax.Prec...  40.1 us
    dot_general x2, matrix products, shards(): jnp.einsum('snk,sbk->snb', picked_cols, current, precision=lax.Precision....  27.8 us
    dot_general x2, matrix products, gradient_blocks(): jnp.einsum('snb,snk->sbk', left_totals, right_samples, precision=lax.Prec...  25 us
  transfers between devices with their start and end apart: 8, of which 7 were waited for; matrix products, arithmetic and copies ran while one was open for 2% of the time, Pallas kernels for 0%

profile of v1, /device:TPU:1, one launch (start us, length us, event | category | flops | bytes accessed | tf_op | source)
XLA Modules:
  0.0 705.8 jit_solution(13332673200302202649)
XLA Ops:
  6.5 0.0 all-gather.6.cloned.1.call-start
  6.5 0.7 all-gather.6.cloned.1.call-update
  7.3 0.0 reduce-scatter.3.cloned.1.call-start
  7.3 0.7 fusion.16
  8.0 0.7 bitcast_select_fusion.2
  8.7 54.9 %all-gather.6.cloned.1.call-done = f32[32,64,128]{2,1,0:T(8,128)} async-done(((f32[4,64,128]{2,1,0:T(8,128)}), f32[32,64,128]{2,1,0:T(8,128)}) %all-gather.6.cloned.1.call-update) | async-done | bytes 1048592 | tf_op jit(solution)/shard_map/all_gather | solution.py:50
  63.6 2.0 gather_fusion
  65.6 14.8 %fusion.3 = f32[100,64,128]{2,1,0:T(8,128)S(1)} fusion(f32[100,64,128]{2,1,0:T(8,128)S(1)} %gather_fusion, f32[1,1,100,128,128]{4,3,2,1,0:T(8,128)} %param.5), kind=kOutput, calls=%fused_computation.12 | convolution fusion | flops 1258291200 | bytes 13107200 | tf_op jit(solution)/shard_map/snk,sbk->snb/dot_general | solution.py:54
  80.4 0.4 slice_bitcast_fusion.1
  80.8 4.1 fusion.7
  84.9 4.4 copy.16
  89.4 0.0 copy-start.5
  89.4 0.0 reduce-scatter.3.cloned.1.call-update
  89.4 0.0 all-gather.10.cloned.1.call-start
  89.4 121.9 %reduce-scatter.3.cloned.1.call-done = f32[4,64,128]{2,1,0:T(8,128)} async-done(((f32[128,64,128]{2,1,0:T(8,128)}), f32[4,64,128]{2,1,0:T(8,128)}) %reduce-scatter.3.cloned.1.call-update) | async-done | bytes 131088 | tf_op jit(solution)/shard_map/reduce_scatter | solution.py:62
  211.3 0.0 all-gather.10.cloned.1.call-update
  211.3 0.0 copy-done.5
  211.4 2.5 stack.2
  213.9 0.0 copy-start.6
  213.9 0.0 copy-start.7
  213.9 9.0 %all-to-all-start = ((f32[32,4,64,128]{3,2,1,0:T(8,128)}), f32[32,4,64,128]{3,2,1,0:T(8,128)}, u32[]{:S(2)}, u32[]{:S(2)}) async-start(f32[32,4,64,128]{3,2,1,0:T(8,128)} %stack.2), calls=%async_computation.1 | async-start | bytes 8388608 | tf_op jit(solution)/shard_map/all_to_all | solution.py:48
  223.0 0.0 all-gather.8.cloned.1.call-start
  223.0 0.5 all-gather.8.cloned.1.call-update
  223.5 0.0 reduce-scatter.5.cloned.1.call-start
  223.6 0.0 copy-done.6
  223.6 0.0 copy-done.7
  223.7 101.1 %all-to-all-done = f32[32,4,64,128]{3,2,1,0:T(8,128)} async-done(((f32[32,4,64,128]{3,2,1,0:T(8,128)}), f32[32,4,64,128]{3,2,1,0:T(8,128)}, u32[]{:S(2)}, u32[]{:S(2)}) %all-to-all-start) | async-done | bytes 4194336 | tf_op jit(solution)/shard_map/all_to_all | solution.py:48
  324.8 4.6 gather_fusion.2
  329.4 0.0 all-gather.10.cloned.1.call-done
  329.4 3.6 gather_fusion.3
  333.1 25.0 %all-gather.8.cloned.1.call-done = f32[128,64,128]{2,1,0:T(8,128)} async-done(((f32[4,64,128]{2,1,0:T(8,128)}), f32[128,64,128]{2,1,0:T(8,128)}) %all-gather.8.cloned.1.call-update) | async-done | bytes 4194320 | tf_op jit(solution)/shard_map/all_gather | solution.py:68
  358.1 4.7 gather_fusion.1
  362.7 0.0 copy-start.1
  362.7 0.0 copy-start.4
  362.7 12.5 %fusion.19 = f32[100,128,128]{2,1,0:T(8,128)S(1)} fusion(f32[100,64,128]{2,1,0:T(8,128)} %gather_fusion.1, f32[100,64,128]{2,1,0:T(8,128)S(1)} %gather_fusion), kind=kOutput, calls=%fused_computation.48 | convolution fusion | flops 1258291200 | bytes 13107200 | tf_op jit(solution)/shard_map/snb,snk->sbk/dot_general | solution.py:12
  375.2 0.0 copy-done.1
  375.2 0.0 copy-done.4
  375.3 19.4 %fusion = f32[100,128,128]{2,1,0:T(8,128)S(1)} fusion(f32[1,1,100,128,128]{4,3,2,1,0:T(8,128)} %param.5, f32[100,128,128]{2,1,0:T(8,128)S(1)} %fusion.19, pred[100]{0:T(512)(128)(4,1)S(1)} %fusion.18, pred[128,128]{1,0:T(8,128)(4,1)S(1)} %iota_compare_fusion, pred[100]{0:T(512)(128)(4,1)S(1)} %bitcast_and_fusion, f32[100,64,128]{2,1,0:T(8,128)S(1)} %copy-done.1, ...), kind=kOutput, calls=%fused_computation.8 | convolution fusion | flops 1282867200 | bytes 26230984 | tf_op jit(solution)/shard_map/snb,snk->sbk/dot_general | solution.py:15
  394.6 0.0 copy-start
  394.7 12.9 %fusion.20 = f32[100,64,128]{2,1,0:T(8,128)S(1)} fusion(f32[100,64,128]{2,1,0:T(8,128)S(1)} %gather_fusion, f32[100,128,128]{2,1,0:T(8,128)S(1)} %fusion), kind=kOutput, calls=%fused_computation.49 | convolution fusion | flops 1258291200 | bytes 13107200 | tf_op jit(solution)/shard_map/snk,sbk->snb/dot_general | solution.py:54
  407.6 0.0 copy-done
  407.6 0.4 slice_bitcast_fusion
  408.0 4.1 fusion.5
  412.1 4.7 copy.18
  416.9 0.0 reduce-scatter.5.cloned.1.call-update
  416.9 0.0 all-gather.14.cloned.1.call-start
  416.9 120.7 %reduce-scatter.5.cloned.1.call-done = f32[4,64,128]{2,1,0:T(8,128)} async-done(((f32[128,64,128]{2,1,0:T(8,128)}), f32[4,64,128]{2,1,0:T(8,128)}) %reduce-scatter.5.cloned.1.call-update) | async-done | bytes 131088 | tf_op jit(solution)/shard_map/reduce_scatter | solution.py:62
  537.6 0.0 all-gather.14.cloned.1.call-update
  537.7 0.0 all-gather.12.cloned.1.call-start
  537.7 0.7 all-gather.12.cloned.1.call-update
  538.4 52.9 %all-gather.14.cloned.1.call-done = f32[32,64,128]{2,1,0:T(8,128)} async-done(((f32[4,64,128]{2,1,0:T(8,128)}), f32[32,64,128]{2,1,0:T(8,128)}) %all-gather.14.cloned.1.call-update) | async-done | bytes 1048592 | tf_op jit(solution)/shard_map/all_gather | solution.py:69
  591.3 3.7 gather_fusion.5
  595.0 65.5 %all-gather.12.cloned.1.call-done = f32[128,64,128]{2,1,0:T(8,128)} async-done(((f32[4,64,128]{2,1,0:T(8,128)}), f32[128,64,128]{2,1,0:T(8,128)}) %all-gather.12.cloned.1.call-update) | async-done | bytes 4194320 | tf_op jit(solution)/shard_map/all_gather | solution.py:68
  660.6 4.7 gather_fusion.4
  665.3 0.0 copy-start.2
  665.3 0.0 copy-start.3
  665.3 12.5 %fusion.21 = f32[100,128,128]{2,1,0:T(8,128)S(1)} fusion(f32[100,64,128]{2,1,0:T(8,128)} %gather_fusion.4, f32[100,64,128]{2,1,0:T(8,128)S(1)} %gather_fusion), kind=kOutput, calls=%fused_computation.50 | convolution fusion | flops 1258291200 | bytes 13107200 | tf_op jit(solution)/shard_map/snb,snk->sbk/dot_general | solution.py:12
  677.8 0.0 copy-done.2
  677.8 0.0 copy-done.3
  677.8 20.7 %fusion.2 = f32[1,1,100,128,128]{4,3,2,1,0:T(8,128)} fusion(f32[100,128,128]{2,1,0:T(8,128)} %copy-done, f32[100,128,128]{2,1,0:T(8,128)S(1)} %fusion.21, pred[100]{0:T(512)(128)(4,1)S(1)} %fusion.18, pred[128,128]{1,0:T(8,128)(4,1)S(1)} %iota_compare_fusion, pred[100]{0:T(512)(128)(4,1)S(1)} %bitcast_and_fusion, f32[100,64,128]{2,1,0:T(8,128)S(1)} %copy-done.2, ...), kind=kOutput, calls=%fused_computation.10 | convolution fusion | flops 1282867200 | bytes 26230984 | tf_op jit(solution)/shard_map/snb,snk->sbk/dot_general | solution.py:15
  (5 shorter events, 0.0 us)
Async XLA Ops:
  6.5 57.0 %all-gather.6.cloned.1.call-start = ((), (), s32[]{:S(2)}) async-start(), calls=%async_computation.3 | async-start | bytes 1179648 | tf_op jit(solution)/shard_map/all_gather | solution.py:50
  7.3 204.1 %reduce-scatter.3.cloned.1.call-start = ((), (), s32[]{:S(2)}) async-start(), calls=%async_computation.4 | async-start | bytes 4325376 | tf_op jit(solution)/shard_map/reduce_scatter | solution.py:62
  89.4 122.0 %copy-start.5 = (f32[4,64,128]{2,1,0:T(8,128)S(1)}, f32[4,64,128]{2,1,0:T(8,128)}, u32[]{:S(2)}) copy-start(f32[4,64,128]{2,1,0:T(8,128)} %param.4) | copy-start | bytes 393220
  89.4 240.0 %all-gather.10.cloned.1.call-start = ((), (), s32[]{:S(2)}) async-start(), calls=%async_computation.6 | async-start | bytes 1179648 | tf_op jit(solution)/shard_map/all_gather | solution.py:69
  213.9 9.7 %copy-start.6 = (s32[1,1,100]{2,1,0:T(1,128)S(1)}, s32[1,1,100]{2,1,0:T(1,128)}, u32[]{:S(2)}) copy-start(s32[1,1,100]{2,1,0:T(1,128)} %param.6) | copy-start | bytes 1204
  213.9 9.7 %copy-start.7 = (s32[1,1,100]{2,1,0:T(1,128)S(1)}, s32[1,1,100]{2,1,0:T(1,128)}, u32[]{:S(2)}) copy-start(s32[1,1,100]{2,1,0:T(1,128)} %param.7) | copy-start | bytes 1204
  213.9 110.9 %all-to-all-start = ((f32[32,4,64,128]{3,2,1,0:T(8,128)}), f32[32,4,64,128]{3,2,1,0:T(8,128)}, u32[]{:S(2)}, u32[]{:S(2)}) async-start(f32[32,4,64,128]{3,2,1,0:T(8,128)} %stack.2), calls=%async_computation.1 | async-start | bytes 8388608 | tf_op jit(solution)/shard_map/all_to_all | solution.py:48
  223.0 135.1 %all-gather.8.cloned.1.call-start = ((), (), s32[]{:S(2)}) async-start(), calls=%async_computation.5 | async-start | bytes 4325376 | tf_op jit(solution)/shard_map/all_gather | solution.py:68
  223.5 314.1 %reduce-scatter.5.cloned.1.call-start = ((), (), s32[]{:S(2)}) async-start(), calls=%async_computation.7 | async-start | bytes 4325376 | tf_op jit(solution)/shard_map/reduce_scatter | solution.py:62
  362.7 12.5 %copy-start.1 = (f32[100,64,128]{2,1,0:T(8,128)S(1)}, f32[100,64,128]{2,1,0:T(8,128)}, u32[]{:S(2)}) copy-start(f32[100,64,128]{2,1,0:T(8,128)} %gather_fusion.2) | copy-start | bytes 9830404
  362.7 12.5 %copy-start.4 = (f32[100,64,128]{2,1,0:T(8,128)S(1)}, f32[100,64,128]{2,1,0:T(8,128)}, u32[]{:S(2)}) copy-start(f32[100,64,128]{2,1,0:T(8,128)} %gather_fusion.3) | copy-start | bytes 9830404
  394.6 13.0 %copy-start = (f32[100,128,128]{2,1,0:T(8,128)}, f32[100,128,128]{2,1,0:T(8,128)S(1)}, u32[]{:S(2)}) copy-start(f32[100,128,128]{2,1,0:T(8,128)S(1)} %fusion) | copy-start | bytes 19660804
  416.9 174.4 %all-gather.14.cloned.1.call-start = ((), (), s32[]{:S(2)}) async-start(), calls=%async_computation.9 | async-start | bytes 1179648 | tf_op jit(solution)/shard_map/all_gather | solution.py:69
  537.7 122.9 %all-gather.12.cloned.1.call-start = ((), (), s32[]{:S(2)}) async-start(), calls=%async_computation.8 | async-start | bytes 4325376 | tf_op jit(solution)/shard_map/all_gather | solution.py:68
  665.3 12.5 %copy-start.2 = (f32[100,64,128]{2,1,0:T(8,128)S(1)}, f32[100,64,128]{2,1,0:T(8,128)}, u32[]{:S(2)}) copy-start(f32[100,64,128]{2,1,0:T(8,128)} %gather_fusion.2) | copy-start | bytes 9830404
  665.3 12.5 %copy-start.3 = (f32[100,64,128]{2,1,0:T(8,128)S(1)}, f32[100,64,128]{2,1,0:T(8,128)}, u32[]{:S(2)}) copy-start(f32[100,64,128]{2,1,0:T(8,128)} %gather_fusion.5) | copy-start | bytes 9830404
Sparse Core Ops, SparseCore 0:
  10.0 53.5 all-gather.5
  89.5 121.7 reduce-scatter.2
  214.0 63.0 all-gather.9
  278.8 79.2 all-gather.7
  417.0 120.5 reduce-scatter.4
  540.1 51.1 all-gather.13
  593.2 67.3 all-gather.11
